TPU v7x, 32 devices: a whole 2x2x4 slice. The times are simulated.
32 devices in a mesh: groups: 2 (over y), ep: 16 (over z, x, core).
Axes of the slice: x: 2, y: 2, z: 4, core: 2. Of those that a mesh axis runs over, the one named last changes fastest.
Arguments:
- tokens: bfloat16 [2048, 2880], P(('groups', 'ep')), parts along dimension 0, may hold values from -6 to 6
- expert_ids: int32 [2048, 4], P(('groups', 'ep')), parts along dimension 0, may hold values from 0 to 15, all different within a row; in each aligned block of 64 rows (0 to 63, 64 to 127, ...) at most 18 rows name the same one
- gate_ints: int32 [2048, 4], P(('groups', 'ep')), parts along dimension 0, may hold values from 1 to 255
- norm_gain: float32 [2880], replicated, may hold values from 0.5 to 2
- weight_in: bfloat16 [16, 2880, 5760], P('ep'), may hold values from -0.109375 to 0.109375
- bias_in: float32 [16, 5760], P('ep'), may hold values from -3 to 3
- weight_out: bfloat16 [16, 2880, 2880], P('ep'), may hold values from -0.109375 to 0.109375
- bias_out: float32 [16, 2880], replicated, may hold values from -3 to 3
Outputs:
- mixed: bfloat16 [2048, 2880], P(('groups', 'ep')), parts along dimension 0
There are 2 independent parts, one for each index of `groups`. A program takes and returns all parts, laid end to end along the dimension named above; an argument that names none is the same for every part. Nothing has to cross between parts.
Inputs may be any that keep to these rules, and one draw needn't show every extreme that they name: `expert_ids`: each row names 4 different experts. Within the rows of one device (aligned blocks of 64 rows) no expert is named more than 18 times.
All inputs are finite; a program needn't handle non-finite values.
Results may differ from a plain program's by a relative error of at most 0.0065.
Values may be sent and summed in bfloat16 or wider, within the bound.
A program may use at most 256 MiB of HBM per device.

v0:
```python
import jax
import jax.numpy as jnp
from jax import lax
from jax.sharding import PartitionSpec as P

CAP = 18


def shards(tokens, expert_ids, gate_ints, norm_gain, weight_in, bias_in, weight_out, bias_out):
    device_count = lax.axis_size("ep")
    expert_count = bias_out.shape[0]
    part_count = device_count // expert_count
    row_count, model_width = tokens.shape
    top_count = expert_ids.shape[1]
    capacity = CAP
    tok_float = tokens.astype(jnp.float32)
    row_scale = lax.rsqrt(jnp.mean(tok_float * tok_float, axis=1, keepdims=True) + 1e-05)
    normed = (tok_float * row_scale * norm_gain[None, :]).astype(jnp.bfloat16)
    int_gates = gate_ints.astype(jnp.float32)
    route_weight = int_gates / jnp.sum(int_gates, axis=1, keepdims=True)
    flat_ids = expert_ids.reshape(row_count * top_count)
    one_hot = (flat_ids[:, None] == jnp.arange(expert_count, dtype=jnp.int32)[None, :]).astype(
        jnp.int32
    )
    slot_rank = jnp.sum((jnp.cumsum(one_hot, axis=0) - one_hot) * one_hot, axis=1)
    slot_target = (flat_ids * capacity + slot_rank).reshape(row_count, top_count)
    slot_ids = jnp.arange(expert_count * capacity, dtype=jnp.int32)
    slot_match = slot_target[None, :, :] == slot_ids[:, None, None]
    picker = jnp.any(slot_match, axis=2).astype(jnp.bfloat16)
    placed = jnp.dot(picker, normed, preferred_element_type=jnp.float32).astype(jnp.bfloat16)
    combiner = jnp.transpose(jnp.sum(jnp.where(slot_match, route_weight[None, :, :], 0.0), axis=2))
    outgoing = jnp.broadcast_to(
        placed.reshape(expert_count, 1, capacity, model_width),
        (expert_count, part_count, capacity, model_width),
    ).reshape(device_count, capacity, model_width)
    arrived = lax.all_to_all(outgoing, "ep", split_axis=0, concat_axis=0, tiled=True)
    source_count = arrived.shape[0]
    slot_count = arrived.shape[1]
    flat_rows = arrived.reshape(source_count * slot_count, model_width)
    pre_act = (
        jnp.dot(flat_rows, weight_in[0], preferred_element_type=jnp.float32) + bias_in[0][None, :]
    )
    half_width = pre_act.shape[1] // 2
    gate_part = pre_act[:, :half_width]
    up_part = pre_act[:, half_width:]
    activated = (gate_part * jax.nn.sigmoid(1.702 * gate_part) * (up_part + 1.0)).astype(
        jnp.bfloat16
    )
    result = jnp.dot(activated, weight_out[0], preferred_element_type=jnp.float32).astype(
        jnp.bfloat16
    )
    returned = lax.all_to_all(
        result.reshape(source_count, slot_count, model_width),
        "ep",
        split_axis=0,
        concat_axis=0,
        tiled=True,
    )
    part_sum = jnp.sum(
        returned.reshape(expert_count, part_count, capacity, model_width), axis=1, dtype=jnp.float32
    ).reshape(expert_count * capacity, model_width)
    moe_rows = jnp.dot(combiner, part_sum, precision=lax.Precision.HIGHEST)
    expert_hot = expert_ids[:, :, None] == jnp.arange(expert_count, dtype=jnp.int32)[None, None, :]
    expert_weight = jnp.sum(jnp.where(expert_hot, route_weight[:, :, None], 0.0), axis=1)
    bias_term = jnp.dot(expert_weight, bias_out, precision=lax.Precision.HIGHEST)
    return (tok_float + moe_rows + bias_term).astype(jnp.bfloat16)


def solution(mesh):
    return jax.shard_map(
        shards,
        mesh=mesh,
        in_specs=(
            P(("groups", "ep"), None),
            P(("groups", "ep"), None),
            P(("groups", "ep"), None),
            P(),
            P("ep", None, None),
            P("ep", None),
            P("ep", None, None),
            P(),
        ),
        out_specs=P(("groups", "ep"), None),
        check_vma=False,
    )
```

profile of v0, /device:TPU:11, one launch (start us, length us, event | category | flops | bytes accessed | tf_op | source)
XLA Modules:
  0.0 163.1 jit_solution(14443241633819949122)
XLA Ops:
  0.0 0.0 copy-start
  0.0 0.8 copy.27
  0.8 0.1 eq.55
  0.9 0.1 eq.51
  1.0 0.6 reduce-window.6
  1.6 0.2 slice_reduce_fusion
  1.9 0.1 fusion.25
  1.9 0.1 reduce_sum.52
  2.1 0.1 copy.30
  2.1 0.7 multiply_add_fusion
  2.8 0.1 fusion.19
  3.0 1.2 fusion.16
  4.1 1.7 %convolution_convert_fusion = bf16[288,2880]{1,0:T(8,128)(2,1)S(1)} fusion(pred[288,64]{0,1:T(8,128)(4,1)S(1)} %fusion.19, bf16[64,2880]{1,0:T(8,128)(2,1)} %param.8, f32[2880]{0:T(1024)} %param.11, f32[64]{0:T(128)S(1)} %add_rsqrt_fusion), kind=kOutput, calls=%fused_computation.6 | convolution fusion | flops 107735040 | bytes 2057728 | tf_op jit(solution)/shard_map/dot_general | solution.py:30
  5.8 0.0 copy-start.2
  5.8 1.7 %reshape_reshape.3 = bf16[16,18,2880]{2,1,0:T(8,128)(2,1)} reshape(bf16[288,2880]{1,0:T(8,128)(2,1)S(1)} %convolution_convert_fusion) | data formatting | bytes 3317760 | tf_op jit(solution)/shard_map/reshape;reshape | solution.py:35
  7.6 6.5 %all-to-all-start = ((bf16[16,18,2880]{2,1,0:T(8,128)(2,1)}), bf16[16,18,2880]{2,1,0:T(8,128)(2,1)S(1)}, u32[]{:S(2)}, u32[]{:S(2)}) async-start(bf16[16,18,2880]{2,1,0:T(8,128)(2,1)} %reshape_reshape.3), calls=%async_computation | async-start | bytes 4521984 | tf_op jit(solution)/shard_map/all_to_all | solution.py:36
  14.1 0.0 copy-done.2
  14.1 0.1 reduce.1
  14.1 50.9 %all-to-all-done = bf16[16,18,2880]{2,1,0:T(8,128)(2,1)S(1)} async-done(((bf16[16,18,2880]{2,1,0:T(8,128)(2,1)}), bf16[16,18,2880]{2,1,0:T(8,128)(2,1)S(1)}, u32[]{:S(2)}, u32[]{:S(2)}) %all-to-all-start) | async-done | bytes 1658912 | tf_op jit(solution)/shard_map/all_to_all | solution.py:36
  65.0 1.8 %reshape.51 = bf16[288,2880]{1,0:T(8,128)(2,1)} reshape(bf16[16,18,2880]{2,1,0:T(8,128)(2,1)S(1)} %all-to-all-done) | data formatting | bytes 3317760 | tf_op jit(solution)/shard_map/reshape | solution.py:39
  66.8 19.5 %fusion.4 = f32[288,5760]{1,0:T(8,128)} fusion(bf16[288,2880]{1,0:T(8,128)(2,1)} %reshape.51, bf16[1,2880,5760]{2,1,0:T(8,128)(2,1)} %param.12, f32[5760]{0:T(1024)S(1)} %reduce.1), kind=kOutput, calls=%fused_computation.4 | convolution fusion | flops 9556807680 | bytes 41495040 | tf_op jit(solution)/shard_map/dot_general | solution.py:41
  86.3 13.2 %fusion.7 = bf16[288,2880]{1,0:T(8,128)(2,1)S(1)} fusion(bf16[1,2880,2880]{2,1,0:T(8,128)(2,1)} %param.14, f32[288,5760]{1,0:T(8,128)} %fusion.4), kind=kOutput, calls=%fused_computation.5 | convolution fusion | flops 4785039360 | bytes 25399296 | tf_op jit(solution)/shard_map/dot_general | solution.py:49
  99.6 0.0 copy-start.4
  99.6 0.0 copy-start.3
  99.6 1.7 %reshape.52 = bf16[16,18,2880]{2,1,0:T(8,128)(2,1)} reshape(bf16[288,2880]{1,0:T(8,128)(2,1)S(1)} %fusion.7) | data formatting | bytes 3317760 | tf_op jit(solution)/shard_map/reshape | solution.py:53
  101.3 0.0 copy-start.1
  101.3 4.9 %all-to-all-start.1 = ((bf16[16,18,2880]{2,1,0:T(8,128)(2,1)}), bf16[16,18,2880]{2,1,0:T(8,128)(2,1)S(1)}, u32[]{:S(2)}, u32[]{:S(2)}) async-start(bf16[16,18,2880]{2,1,0:T(8,128)(2,1)} %reshape.52), calls=%async_computation.1 | async-start | bytes 4521984 | tf_op jit(solution)/shard_map/all_to_all | solution.py:52
  106.2 0.0 copy-done.4
  106.2 0.0 copy-done.3
  106.3 0.1 select_reduce_fusion
  106.4 50.7 %all-to-all-done.1 = bf16[16,18,2880]{2,1,0:T(8,128)(2,1)S(1)} async-done(((bf16[16,18,2880]{2,1,0:T(8,128)(2,1)}), bf16[16,18,2880]{2,1,0:T(8,128)(2,1)S(1)}, u32[]{:S(2)}, u32[]{:S(2)}) %all-to-all-start.1) | async-done | bytes 1658912 | tf_op jit(solution)/shard_map/all_to_all | solution.py:52
  157.1 1.8 %reshape.53 = bf16[288,2880]{1,0:T(8,128)(2,1)} reshape(bf16[16,18,2880]{2,1,0:T(8,128)(2,1)S(1)} %all-to-all-done.1) | data formatting | bytes 3317760 | tf_op jit(solution)/shard_map/reshape | solution.py:61
  158.9 0.0 copy-done.1
  158.9 2.6 %convolution_add_fusion.1 = f32[64,2880]{1,0:T(8,128)S(1)} fusion(f32[288,64]{0,1:T(8,128)S(1)} %select_reduce_fusion, bf16[288,2880]{1,0:T(8,128)(2,1)} %reshape.53, bf16[64,2880]{1,0:T(8,128)(2,1)S(1)} %copy-done.1), kind=kOutput, calls=%fused_computation.8 | convolution fusion | flops 637378560 | bytes 2838528 | tf_op jit(solution)/shard_map/dot_general | solution.py:62
  161.6 0.0 copy-done
  161.6 1.6 fusion.10
  (7 shorter events, 0.1 us)
Async XLA Ops:
  0.0 161.6 %copy-start = (f32[16,2880]{1,0:T(8,128)S(1)}, f32[16,2880]{1,0:T(8,128)}, u32[]{:S(2)}) copy-start(f32[16,2880]{1,0:T(8,128)} %param.15) | copy-start | bytes 552964
  5.8 8.2 %copy-start.2 = (f32[1,5760]{1,0:T(1,128)S(1)}, f32[1,5760]{1,0:T(1,128)}, u32[]{:S(2)}) copy-start(f32[1,5760]{1,0:T(1,128)} %param.13) | copy-start | bytes 69124
  7.6 57.5 %all-to-all-start = ((bf16[16,18,2880]{2,1,0:T(8,128)(2,1)}), bf16[16,18,2880]{2,1,0:T(8,128)(2,1)S(1)}, u32[]{:S(2)}, u32[]{:S(2)}) async-start(bf16[16,18,2880]{2,1,0:T(8,128)(2,1)} %reshape_reshape.3), calls=%async_computation | async-start | bytes 4521984 | tf_op jit(solution)/shard_map/all_to_all | solution.py:36
  99.6 6.6 %copy-start.4 = (s32[64,4]{0,1:T(4,128)S(1)}, s32[64,4]{0,1:T(4,128)}, u32[]{:S(2)}) copy-start(s32[64,4]{0,1:T(4,128)} %param.10) | copy-start | bytes 3076
  99.6 6.7 %copy-start.3 = (s32[64,4]{0,1:T(4,128)S(1)}, s32[64,4]{0,1:T(4,128)}, u32[]{:S(2)}) copy-start(s32[64,4]{0,1:T(4,128)} %param.9) | copy-start | bytes 3076
  101.3 57.6 %copy-start.1 = (bf16[64,2880]{1,0:T(8,128)(2,1)S(1)}, bf16[64,2880]{1,0:T(8,128)(2,1)}, u32[]{:S(2)}) copy-start(bf16[64,2880]{1,0:T(8,128)(2,1)} %param.8) | copy-start | bytes 1105924
  101.3 55.8 %all-to-all-start.1 = ((bf16[16,18,2880]{2,1,0:T(8,128)(2,1)}), bf16[16,18,2880]{2,1,0:T(8,128)(2,1)S(1)}, u32[]{:S(2)}, u32[]{:S(2)}) async-start(bf16[16,18,2880]{2,1,0:T(8,128)(2,1)} %reshape.52), calls=%async_computation.1 | async-start | bytes 4521984 | tf_op jit(solution)/shard_map/all_to_all | solution.py:52
where the time goes:
time: 163 us
  waiting for transfers between devices  102 us (63%)
  matrix products  38.6 us (24%)
  starting transfers between devices  11.4 us (7%)
  local copies, waits for them, and re-layouts  8.44 us (5%)
  other arithmetic  2.94 us (2%)
    all_to_all x1, waiting for transfers between devices, shards(): lax.all_to_all(outgoing, 'ep', split_axis=0, concat_axis=0, tiled=True)  50.9 us
    all_to_all x1, waiting for transfers between devices, shards(): lax.all_to_all(result.reshape(source_count, slot_count, model_width), 'ep...  50.7 us
    dot_general x1, matrix products, shards(): jnp.dot(flat_rows, weight_in[0], preferred_element_type=jnp.float32)  19.5 us
    dot_general x1, matrix products, shards(): jnp.dot(activated, weight_out[0], preferred_element_type=jnp.float32)  13.2 us
    all_to_all x1, starting transfers between devices, shards(): lax.all_to_all(outgoing, 'ep', split_axis=0, concat_axis=0, tiled=True)  6.52 us
    all_to_all x1, starting transfers between devices, shards(): lax.all_to_all(result.reshape(source_count, slot_count, model_width), 'ep...  4.91 us
  transfers between devices with their start and end apart: 2, of which 2 were waited for; matrix products, arithmetic and copies ran while one was open for 0% of the time, Pallas kernels for 0%

commit v1 on v0

--- a/solution.py
+++ b/solution.py
@@ -1,9 +1,485 @@
+import functools
+
 import jax
 import jax.numpy as jnp
 from jax import lax
+from jax.experimental import pallas as pl
+from jax.experimental.pallas import tpu as pltpu
 from jax.sharding import PartitionSpec as P
 
 CAP = 18
+PLANE = 4
+LANES = 128
+MESH = pl.DeviceIdType.MESH
+VMEM_ROOM = 66_000_000
+
+
+def round_up(value, step):
+    return -(-value // step) * step
+
+
+def expert_kernel(
+    dims,
+    normed_ref,
+    meta_ref,
+    pick_ref,
+    gate_ref,
+    mark_ref,
+    inv_ref,
+    weight_ref,
+    bias_out_ref,
+    bias_in_ref,
+    w_in_ref,
+    w_out_ref,
+    out_ref,
+    *scratch,
+):
+    depth, rows, width, half, slots, cols = dims
+    count = len(cols)
+    scratch = list(scratch)
+
+    def take(n):
+        got = scratch[:n]
+        del scratch[:n]
+        return got
+
+    gathered = take(count)
+    sending = take(count)
+    landed = take(count)
+    answers = take(count)
+    from_above = take(count)
+    from_below = take(count)
+    (meta_all, select, combine, dense, acc, act, w_buf, w_out) = take(8)
+    (w_sem, w_out_sem) = take(2)
+    (up_send, down_send, chain_recv) = take(3)
+    (side_send, side_recv, back_send, back_recv) = take(4)
+    (ret_up_send, ret_down_send, ret_up_recv, ret_down_recv) = take(4)
+
+    me = lax.axis_index("ep")
+    level = me // PLANE
+    seat = me % PLANE
+    has_up = level < depth - 1
+    has_down = level > 0
+    starts = [sum(c for c, _ in cols[:k]) for k in range(count)]
+
+    def w_copy(k):
+        real = cols[k][1]
+        return pltpu.make_async_copy(
+            w_in_ref.at[0, pl.ds(starts[k], real), :],
+            w_buf.at[k % 2, pl.ds(0, real), :],
+            w_sem.at[k],
+        )
+
+    out_copy = pltpu.make_async_copy(w_out_ref.at[0], w_out, w_out_sem)
+    w_copy(0).start()
+    if count > 1:
+        w_copy(1).start()
+    out_copy.start()
+
+    barrier = pltpu.get_barrier_semaphore()
+    for step in range(1, PLANE):
+        pl.semaphore_signal(
+            barrier,
+            inc=1,
+            device_id={"ep": level * PLANE + lax.rem(seat + step, PLANE)},
+            device_id_type=MESH,
+        )
+
+    @pl.when(has_up)
+    def _():
+        pl.semaphore_signal(barrier, inc=1, device_id={"ep": me + PLANE}, device_id_type=MESH)
+
+    @pl.when(has_down)
+    def _():
+        pl.semaphore_signal(barrier, inc=1, device_id={"ep": me - PLANE}, device_id_type=MESH)
+
+    peers = PLANE - 1 + has_up.astype(jnp.int32) + has_down.astype(jnp.int32)
+    pl.semaphore_wait(barrier, peers)
+
+    def block(k, z):
+        buf = meta_all if k == 0 else gathered[k - 1]
+        return buf.at[pl.ds(pl.multiple_of(z * rows, rows), rows), :]
+
+    def chain(k, z, own, sem, target):
+        if own:
+            src = meta_ref if k == 0 else normed_ref.at[:, pl.ds(starts[k - 1], cols[k - 1][0])]
+        else:
+            src = block(k, z)
+        return pltpu.make_async_remote_copy(
+            src_ref=src,
+            dst_ref=block(k, z),
+            send_sem=sem.at[k, z],
+            recv_sem=chain_recv.at[k, z],
+            device_id={"ep": target},
+            device_id_type=MESH,
+        )
+
+    def send_own(k):
+        @pl.when(has_up)
+        def _():
+            chain(k, level, True, up_send, me + PLANE).start()
+
+        @pl.when(has_down)
+        def _():
+            chain(k, level, True, down_send, me - PLANE).start()
+
+    def relay(k):
+        for far in range(1, depth):
+            below = level - far
+
+            @pl.when(below >= 0)
+            def _():
+                chain(k, below, False, up_send, me).wait_recv()
+
+                @pl.when(has_up)
+                def _():
+                    chain(k, below, False, up_send, me + PLANE).start()
+
+            above = level + far
+
+            @pl.when(above < depth)
+            def _():
+                chain(k, above, False, down_send, me).wait_recv()
+
+                @pl.when(has_down)
+                def _():
+                    chain(k, above, False, down_send, me - PLANE).start()
+
+    def drain_chain(k):
+        for z in range(depth):
+
+            @pl.when(jnp.logical_and(has_up, z <= level))
+            def _():
+                chain(k, z, False, up_send, me + PLANE).wait_send()
+
+            @pl.when(jnp.logical_and(has_down, z >= level))
+            def _():
+                chain(k, z, False, down_send, me - PLANE).wait_send()
+
+    def seat_rows(buf, s):
+        return buf.at[pl.ds(pl.multiple_of(s * slots, 16), slots), :]
+
+    def side(k, step, src, dst, send, recv):
+        peer = lax.rem(seat + step, PLANE)
+        return pltpu.make_async_remote_copy(
+            src_ref=seat_rows(src[k], peer),
+            dst_ref=seat_rows(dst[k], seat),
+            send_sem=send.at[k, step],
+            recv_sem=recv.at[k, step],
+            device_id={"ep": level * PLANE + peer},
+            device_id_type=MESH,
+        )
+
+    def side_all(k, src, dst, send, recv):
+        for step in range(1, PLANE):
+            side(k, step, src, dst, send, recv).start()
+        mine = pl.ds(pl.multiple_of(seat * slots, 16), slots)
+        dst[k][mine, :] = src[k][mine, :]
+
+    def first_matmul(k):
+        real = cols[k][1]
+        for step in range(1, PLANE):
+            side(k, step, sending, landed, side_send, side_recv).wait_recv()
+        w_copy(k).wait()
+        x_ref = landed[k]
+
+        def tile(start, size):
+            part = jnp.dot(
+                x_ref[:, :real],
+                w_buf[k % 2, :real, pl.ds(start, size)],
+                preferred_element_type=jnp.float32,
+            )
+            if k == 0:
+                acc[:, pl.ds(start, size)] = part + bias_in_ref[:, pl.ds(start, size)]
+            else:
+                acc[:, pl.ds(start, size)] += part
+
+        total = 2 * half
+        size = 512
+        full = total // size
+
+        @pl.loop(0, full)
+        def _(i):
+            tile(pl.multiple_of(i * size, size), size)
+
+        if total % size:
+            tile(full * size, total % size)
+        if k + 2 < count:
+            w_copy(k + 2).start()
+
+    send_own(0)
+    send_own(1)
+    own = pl.ds(pl.multiple_of(level * rows, rows), rows)
+    meta_all[own, :] = meta_ref[...]
+    for k in range(count):
+        gathered[k][own, :] = normed_ref[:, starts[k] : starts[k] + cols[k][0]]
+    relay(0)
+    table = meta_all[...]
+    rank = jnp.dot(table, pick_ref[...], preferred_element_type=jnp.float32)
+    gate = jnp.dot(table, gate_ref[...], preferred_element_type=jnp.float32)
+    hit = rank == mark_ref[...]
+    combine[...] = jnp.where(hit, gate, 0.0).astype(jnp.bfloat16)
+    select[...] = jnp.transpose(jnp.where(hit, 1.0, 0.0)).astype(jnp.bfloat16)
+
+    for k in range(count):
+        if k + 2 <= count:
+            send_own(k + 2)
+        relay(k + 1)
+        sending[k][...] = jnp.dot(
+            select[: PLANE * slots, :], gathered[k][...], preferred_element_type=jnp.float32
+        ).astype(jnp.bfloat16)
+        side_all(k, sending, landed, side_send, side_recv)
+        if k > 0:
+            first_matmul(k - 1)
+    first_matmul(count - 1)
+
+    part_rows = 32
+
+    @pl.loop(0, PLANE * slots // part_rows)
+    def _(i):
+        here = pl.ds(pl.multiple_of(i * part_rows, part_rows), part_rows)
+        for start in range(0, half, 384):
+            size = min(384, half - start)
+            g = acc[here, start : start + size]
+            u = acc[here, half + start : half + start + size]
+            act[here, start : start + size] = (
+                g * jax.nn.sigmoid(1.702 * g) * (u + 1.0)
+            ).astype(jnp.bfloat16)
+
+    for k in range(count + 1):
+        drain_chain(k)
+    for k in range(count):
+        for step in range(1, PLANE):
+            side(k, step, sending, landed, side_send, side_recv).wait_send()
+    out_copy.wait()
+
+    def second_matmul(k):
+        real = cols[k][1]
+        size = 256
+
+        def tile(start, at, n):
+            sending[k][:, pl.ds(at, n)] = jnp.dot(
+                act[...], w_out[:, pl.ds(start, n)], preferred_element_type=jnp.float32
+            ).astype(jnp.bfloat16)
+
+        full = real // size
+
+        @pl.loop(0, full)
+        def _(i):
+            at = pl.multiple_of(i * size, size)
+            tile(starts[k] + at, at, size)
+
+        if real % size:
+            tile(starts[k] + full * size, full * size, real % size)
+        side_all(k, sending, answers, back_send, back_recv)
+
+    def ret(k, z, land, send, recv, target):
+        there = pl.ds(pl.multiple_of(z * rows, rows), rows)
+        return pltpu.make_async_remote_copy(
+            src_ref=gathered[k].at[there, :],
+            dst_ref=land[k].at[there, :],
+            send_sem=send.at[k, z],
+            recv_sem=recv.at[k, z],
+            device_id={"ep": target},
+            device_id_type=MESH,
+        )
+
+    def pass_on(k, z, land, send, recv, target, more):
+        there = pl.ds(z * rows, rows)
+
+        @pl.when(more)
+        def _():
+            ret(k, z, land, send, recv, target).wait_recv()
+            gathered[k][there, :] = (
+                dense[there, : cols[k][0]] + land[k][there, :].astype(jnp.float32)
+            ).astype(jnp.bfloat16)
+
+        @pl.when(jnp.logical_not(more))
+        def _():
+            gathered[k][there, :] = dense[there, : cols[k][0]].astype(jnp.bfloat16)
+
+        ret(k, z, land, send, recv, target).start()
+
+    def reduce(k):
+        for step in range(1, PLANE):
+            side(k, step, sending, answers, back_send, back_recv).wait_recv()
+        wide, real = cols[k]
+        dense[:, :wide] = jnp.dot(
+            combine[:, : PLANE * slots], answers[k][...], preferred_element_type=jnp.float32
+        )
+        for far in range(depth - 1):
+            low, high = far, depth - 1 - far
+
+            @pl.when(low < level)
+            def _():
+                pass_on(k, low, from_above, ret_down_send, ret_down_recv, me - PLANE, has_up)
+
+            @pl.when(high > level)
+            def _():
+                pass_on(k, high, from_below, ret_up_send, ret_up_recv, me + PLANE, has_down)
+
+    def finish(k):
+        wide, real = cols[k]
+
+        @pl.when(has_up)
+        def _():
+            ret(k, level, from_above, ret_down_send, ret_down_recv, me).wait_recv()
+
+        @pl.when(has_down)
+        def _():
+            ret(k, level, from_below, ret_up_send, ret_up_recv, me).wait_recv()
+
+        @pl.when(has_up)
+        def _():
+            home[k % 2, :, :wide] += from_above[k][own, :].astype(jnp.float32)
+
+        @pl.when(has_down)
+        def _():
+            home[k % 2, :, :wide] += from_below[k][own, :].astype(jnp.float32)
+
+        here = slice(starts[k], starts[k] + real)
+        out_ref[:, here] = home[k % 2, :, :real] * inv_ref[...] + jnp.dot(
+            weight_ref[...],
+            bias_out_ref[:, here],
+            preferred_element_type=jnp.float32,
+            precision=lax.Precision.HIGHEST,
+        )
+
+    (home,) = take(1)
+    for k in range(count):
+        second_matmul(k)
+        if k > 0:
+            reduce(k - 1)
+            home[(k - 1) % 2, :, : cols[k - 1][0]] = dense[own, : cols[k - 1][0]]
+            if k > 1:
+                finish(k - 2)
+    last = count - 1
+    reduce(last)
+    home[last % 2, :, : cols[last][0]] = dense[own, : cols[last][0]]
+    if last > 0:
+        finish(last - 1)
+    finish(last)
+
+    for k in range(count):
+        for step in range(1, PLANE):
+            side(k, step, sending, answers, back_send, back_recv).wait_send()
+        for z in range(depth):
+
+            @pl.when(z < level)
+            def _():
+                ret(k, z, from_above, ret_down_send, ret_down_recv, me - PLANE).wait_send()
+
+            @pl.when(z > level)
+            def _():
+                ret(k, z, from_below, ret_up_send, ret_up_recv, me + PLANE).wait_send()
+
+
+def fused(tokens, expert_ids, gate_ints, norm_gain, weight_in, bias_in, weight_out, bias_out):
+    size = lax.axis_size("ep")
+    rows, width = tokens.shape
+    experts = bias_out.shape[0]
+    half = weight_out.shape[1]
+    depth = size // PLANE
+    slots = round_up(depth * CAP, 16)
+    padded = round_up(width, LANES)
+    cols = []
+    while sum(c for c, _ in cols) < padded:
+        at = sum(c for c, _ in cols)
+        cols.append((min(768, padded - at), min(768, width - at)))
+    cols = tuple(cols)
+    count = len(cols)
+    lane_slots = round_up(PLANE * slots, LANES)
+
+    tok_float = tokens.astype(jnp.float32)
+    row_scale = lax.rsqrt(jnp.mean(tok_float * tok_float, axis=1, keepdims=True) + 1e-05)
+    normed = (tok_float * row_scale * norm_gain[None, :]).astype(jnp.bfloat16)
+    normed = jnp.pad(normed, ((0, 0), (0, padded - width)))
+    gates = gate_ints.astype(jnp.float32)
+    inv = 1.0 / jnp.sum(gates, axis=1, keepdims=True)
+    names = jnp.arange(experts, dtype=jnp.int32)
+    hot = expert_ids[:, :, None] == names[None, None, :]
+    chosen = jnp.any(hot, axis=1)
+    gate_of = jnp.sum(jnp.where(hot, gates[:, :, None], 0.0), axis=1)
+    expert_weight = gate_of * inv
+    lower = jnp.tril(jnp.ones((rows, rows), jnp.bfloat16))
+    rank = jnp.dot(lower, chosen.astype(jnp.bfloat16), preferred_element_type=jnp.float32)
+    rank = jnp.where(chosen, rank, 0.0)
+    gap = jnp.zeros((rows, LANES // 2 - experts), jnp.float32)
+    meta = jnp.concatenate([rank, gap, gate_of, gap], axis=1).astype(jnp.bfloat16)
+
+    level = lax.axis_index("ep") // PLANE
+    slot = jnp.arange(lane_slots, dtype=jnp.int32)
+    inside = slot % slots
+    target = level * PLANE + slot // slots
+    valid = (slot < PLANE * slots) & (inside < depth * CAP)
+    lane = jnp.arange(LANES, dtype=jnp.int32)[:, None]
+    pick = ((lane == target[None, :]) & valid[None, :]).astype(jnp.bfloat16)
+    gate_pick = ((lane == LANES // 2 + target[None, :]) & valid[None, :]).astype(jnp.bfloat16)
+    row_level = jnp.arange(depth * rows, dtype=jnp.int32)[:, None] // rows
+    mark = jnp.where(
+        valid[None, :] & (row_level == (inside // CAP)[None, :]),
+        (inside % CAP + 1)[None, :],
+        -1,
+    ).astype(jnp.float32)
+
+    bf16, f32 = jnp.bfloat16, jnp.float32
+    all_rows, all_slots = depth * rows, PLANE * slots
+    dma = pltpu.SemaphoreType.DMA
+
+    def wide(n):
+        return [pltpu.VMEM((n, c), bf16) for c, _ in cols]
+
+    scratch = (
+        wide(all_rows)
+        + wide(all_slots)
+        + wide(all_slots)
+        + wide(all_slots)
+        + wide(all_rows)
+        + wide(all_rows)
+        + [
+            pltpu.VMEM((all_rows, LANES), bf16),
+            pltpu.VMEM((lane_slots, all_rows), bf16),
+            pltpu.VMEM((all_rows, lane_slots), bf16),
+            pltpu.VMEM((all_rows, cols[0][0]), f32),
+            pltpu.VMEM((all_slots, 2 * half), f32),
+            pltpu.VMEM((all_slots, half), bf16),
+            pltpu.VMEM((2, cols[0][0], 2 * half), bf16),
+            pltpu.VMEM((half, width), bf16),
+            dma((count,)),
+            dma,
+            dma((count + 1, depth)),
+            dma((count + 1, depth)),
+            dma((count + 1, depth)),
+        ]
+        + [dma((count, PLANE))] * 4
+        + [dma((count, depth))] * 4
+        + [pltpu.VMEM((2, rows, cols[0][0]), f32)]
+    )
+    vmem = pl.BlockSpec(memory_space=pltpu.VMEM)
+    hbm = pl.BlockSpec(memory_space=pl.ANY)
+    moe = pl.pallas_call(
+        functools.partial(expert_kernel, (depth, rows, width, half, slots, cols)),
+        out_shape=jax.ShapeDtypeStruct((rows, width), f32),
+        in_specs=[vmem] * 9 + [hbm] * 2,
+        out_specs=vmem,
+        scratch_shapes=scratch,
+        compiler_params=pltpu.CompilerParams(
+            collective_id=0, has_side_effects=True, vmem_limit_bytes=VMEM_ROOM
+        ),
+    )(
+        normed,
+        meta,
+        pick,
+        gate_pick,
+        mark,
+        inv,
+        expert_weight,
+        bias_out,
+        bias_in,
+        weight_in,
+        weight_out,
+    )
+    return (tok_float + moe).astype(jnp.bfloat16)
 
 
 def shards(tokens, expert_ids, gate_ints, norm_gain, weight_in, bias_in, weight_out, bias_out):
@@ -66,9 +542,19 @@
     return (tok_float + moe_rows + bias_term).astype(jnp.bfloat16)
 
 
+def layer(*arrays):
+    weight_in, weight_out, bias_out = arrays[4], arrays[6], arrays[7]
+    device_count = lax.axis_size("ep")
+    one_each = device_count == bias_out.shape[0] and device_count % PLANE == 0
+    held = 2 * weight_out.shape[1] * (2 * 2 * 768 + weight_out.shape[2])
+    if one_each and 2 * held < 3 * VMEM_ROOM and bias_out.shape[0] <= LANES // 2:
+        return fused(*arrays)
+    return shards(*arrays)
+
+
 def solution(mesh):
     return jax.shard_map(
-        shards,
+        layer,
         mesh=mesh,
         in_specs=(
             P(("groups", "ep"), None),

time: 163 us -> 125 us (0.77)
  the two profiles are of different devices: /device:TPU:11 before, /device:TPU:0 now
where the time goes in v1:
time: 125 us; the launch traced here: 123 us
  Pallas kernels  111 us (89%)
  other arithmetic  10.1 us (8%)
  local copies, waits for them, and re-layouts  1.75 us (1%)
    pallas_call x1, Pallas kernels, fused(): pl.pallas_call(functools.partial(expert_kernel, (depth, rows, width, half...  111 us

profile of v1, /device:TPU:0, one launch (start us, length us, event | category | flops | bytes accessed | tf_op | source)
XLA Modules:
  0.0 123.0 jit_solution(17928547645514861245)
XLA Ops:
  0.0 0.0 copy-start
  0.0 0.7 convert_reduce_fusion
  0.8 1.2 fusion.1
  2.0 0.7 fusion.9
  2.7 0.7 convert_element_type.27
  3.4 0.7 select_reduce_fusion
  4.1 0.1 copy.18
  4.2 0.1 fusion
  4.3 0.1 copy.20
  4.4 0.7 pad_maximum_fusion.meta_ref
  5.1 0.1 copy.21
  5.2 0.7 broadcast_multiply_fusion.weight_ref
  5.9 0.7 copy.23.inv_ref
  6.6 0.7 fusion.8
  7.3 1.1 fusion.3
  8.5 0.8 pad.4.normed_ref
  9.2 0.9 select_convert_fusion.mark_ref
  10.1 110.9 %shard_map.82 = f32[64,2880]{1,0:T(8,128)} custom-call(bf16[64,2944]{1,0:T(8,128)(2,1)} %pad.4.normed_ref, bf16[64,128]{1,0:T(8,128)(2,1)} %pad_maximum_fusion.meta_ref, bf16[128,384]{1,0:T(8,128)(2,1)} %get-tuple-element.6.pick_ref, bf16[128,384]{1,0:T(8,128)(2,1)} %get-tuple-element.5.gate_ref, f32[256,384]{1,0:T(8,128)} %select_convert_fusion.mark_ref, ...), custom_call_target="tpu_custom_call" | custom-call | tf_op jit(solution)/shard_map/pallas_call | solution.py:460
  121.0 0.0 copy-done
  121.0 1.9 %fusion.4 = bf16[64,2880]{1,0:T(8,128)(2,1)} fusion(f32[64,2880]{1,0:T(8,128)} %shard_map.82, bf16[64,2880]{1,0:T(8,128)(2,1)S(1)} %copy-done), kind=kLoop, calls=%fused_computation.8 | loop fusion | flops 552960 | bytes 1474560 | tf_op jit(solution)/shard_map/convert_element_type | solution.py:482
  (9 shorter events, 0.1 us)
Async XLA Ops:
  0.0 121.0 %copy-start = (bf16[64,2880]{1,0:T(8,128)(2,1)S(1)}, bf16[64,2880]{1,0:T(8,128)(2,1)}, u32[]{:S(2)}) copy-start(bf16[64,2880]{1,0:T(8,128)(2,1)} %param.8) | copy-start | bytes 1105924

commit v2 on v1

--- a/solution.py
+++ b/solution.py
@@ -2,6 +2,7 @@
 
 import jax
 import jax.numpy as jnp
+import numpy as np
 from jax import lax
 from jax.experimental import pallas as pl
 from jax.experimental.pallas import tpu as pltpu
@@ -20,13 +21,11 @@
 
 def expert_kernel(
     dims,
-    normed_ref,
-    meta_ref,
-    pick_ref,
-    gate_ref,
-    mark_ref,
-    inv_ref,
-    weight_ref,
+    tokens_ref,
+    ids_ref,
+    gates_ref,
+    gain_ref,
+    slot_ref,
     bias_out_ref,
     bias_in_ref,
     w_in_ref,
@@ -47,19 +46,22 @@
     sending = take(count)
     landed = take(count)
     answers = take(count)
-    from_above = take(count)
-    from_below = take(count)
+    relayed = take(count)
+    home_in = take(count)
     (meta_all, select, combine, dense, acc, act, w_buf, w_out) = take(8)
+    (normed_ref, meta_ref) = take(2)
     (w_sem, w_out_sem) = take(2)
-    (up_send, down_send, chain_recv) = take(3)
+    (own_send, pass_send, chain_recv) = take(3)
     (side_send, side_recv, back_send, back_recv) = take(4)
-    (ret_up_send, ret_down_send, ret_up_recv, ret_down_recv) = take(4)
+    (ret_send, ret_recv, home_recv) = take(3)
 
     me = lax.axis_index("ep")
     level = me // PLANE
     seat = me % PLANE
     has_up = level < depth - 1
     has_down = level > 0
+    near = [(d - 1, level + d < depth, me + d * PLANE) for d in (2, 1) if d < depth]
+    near += [(d + 1, level - d >= 0, me - d * PLANE) for d in (2, 1) if d < depth]
     starts = [sum(c for c, _ in cols[:k]) for k in range(count)]
 
     def w_copy(k):
@@ -74,7 +76,6 @@
     w_copy(0).start()
     if count > 1:
         w_copy(1).start()
-    out_copy.start()
 
     barrier = pltpu.get_barrier_semaphore()
     for step in range(1, PLANE):
@@ -85,22 +86,48 @@
             device_id_type=MESH,
         )
 
-    @pl.when(has_up)
-    def _():
-        pl.semaphore_signal(barrier, inc=1, device_id={"ep": me + PLANE}, device_id_type=MESH)
-
-    @pl.when(has_down)
-    def _():
-        pl.semaphore_signal(barrier, inc=1, device_id={"ep": me - PLANE}, device_id_type=MESH)
-
-    peers = PLANE - 1 + has_up.astype(jnp.int32) + has_down.astype(jnp.int32)
+    peers = PLANE - 1
+    for _, present, device in near:
+        peers = peers + present.astype(jnp.int32)
+
+        @pl.when(present)
+        def _():
+            pl.semaphore_signal(barrier, inc=1, device_id={"ep": device}, device_id_type=MESH)
+
+    bf16, f32 = jnp.bfloat16, jnp.float32
+    experts = bias_out_ref.shape[0]
+    lane = lax.broadcasted_iota(jnp.int32, (rows, LANES), 1)
+    gates = gates_ref[...].astype(f32)
+    inv = 1.0 / jnp.sum(gates, axis=1, keepdims=True)
+    chosen = jnp.zeros((rows, LANES), f32)
+    gate_of = jnp.zeros((rows, LANES), f32)
+    gate_lane = jnp.zeros((rows, LANES), f32)
+    for entry in range(ids_ref.shape[1]):
+        name = ids_ref[:, entry : entry + 1]
+        value = gates[:, entry : entry + 1]
+        chosen += jnp.where(lane == name, 1.0, 0.0)
+        gate_of += jnp.where(lane == name, value, 0.0)
+        gate_lane += jnp.where(lane == name + LANES // 2, value, 0.0)
+    lower = jnp.where(
+        lax.broadcasted_iota(jnp.int32, (rows, rows), 0)
+        >= lax.broadcasted_iota(jnp.int32, (rows, rows), 1),
+        1.0,
+        0.0,
+    ).astype(bf16)
+    rank = jnp.dot(lower, chosen.astype(bf16), preferred_element_type=f32)
+    meta_ref[...] = (rank * chosen + gate_lane).astype(bf16)
+    tok = tokens_ref[...].astype(f32)
+    scale = lax.rsqrt(jnp.sum(tok * tok, axis=1, keepdims=True) * (1.0 / width) + 1e-05)
+    normed_ref[:, :width] = (tok * scale * gain_ref[...]).astype(bf16)
+    if normed_ref.shape[1] > width:
+        normed_ref[:, width:] = jnp.zeros((rows, normed_ref.shape[1] - width), bf16)
     pl.semaphore_wait(barrier, peers)
 
     def block(k, z):
         buf = meta_all if k == 0 else gathered[k - 1]
         return buf.at[pl.ds(pl.multiple_of(z * rows, rows), rows), :]
 
-    def chain(k, z, own, sem, target):
+    def chain(k, z, own, sem, at, target):
         if own:
             src = meta_ref if k == 0 else normed_ref.at[:, pl.ds(starts[k - 1], cols[k - 1][0])]
         else:
@@ -108,53 +135,47 @@
         return pltpu.make_async_remote_copy(
             src_ref=src,
             dst_ref=block(k, z),
-            send_sem=sem.at[k, z],
+            send_sem=sem.at[k, at],
             recv_sem=chain_recv.at[k, z],
             device_id={"ep": target},
             device_id_type=MESH,
         )
 
     def send_own(k):
-        @pl.when(has_up)
-        def _():
-            chain(k, level, True, up_send, me + PLANE).start()
-
-        @pl.when(has_down)
-        def _():
-            chain(k, level, True, down_send, me - PLANE).start()
+        for slot, present, device in near:
+
+            @pl.when(present)
+            def _():
+                chain(k, level, True, own_send, slot, device).start()
 
     def relay(k):
-        for far in range(1, depth):
-            below = level - far
-
-            @pl.when(below >= 0)
-            def _():
-                chain(k, below, False, up_send, me).wait_recv()
-
-                @pl.when(has_up)
+        for far in [*range(2, depth), 1]:
+            for z, on, device in (
+                (level - far, has_up, me + PLANE),
+                (level + far, has_down, me - PLANE),
+            ):
+
+                @pl.when(jnp.logical_and(z >= 0, z < depth))
                 def _():
-                    chain(k, below, False, up_send, me + PLANE).start()
-
-            above = level + far
-
-            @pl.when(above < depth)
-            def _():
-                chain(k, above, False, down_send, me).wait_recv()
-
-                @pl.when(has_down)
-                def _():
-                    chain(k, above, False, down_send, me - PLANE).start()
+                    chain(k, z, False, pass_send, z, me).wait_recv()
+                    if far > 1:
+
+                        @pl.when(on)
+                        def _():
+                            chain(k, z, False, pass_send, z, device).start()
 
     def drain_chain(k):
+        for slot, present, device in near:
+
+            @pl.when(present)
+            def _():
+                chain(k, level, True, own_send, slot, device).wait_send()
+
         for z in range(depth):
 
-            @pl.when(jnp.logical_and(has_up, z <= level))
-            def _():
-                chain(k, z, False, up_send, me + PLANE).wait_send()
-
-            @pl.when(jnp.logical_and(has_down, z >= level))
-            def _():
-                chain(k, z, False, down_send, me - PLANE).wait_send()
+            @pl.when(jnp.logical_or(has_up & (z <= level - 2), has_down & (z >= level + 2)))
+            def _():
+                chain(k, z, False, pass_send, z, me).wait_send()
 
     def seat_rows(buf, s):
         return buf.at[pl.ds(pl.multiple_of(s * slots, 16), slots), :]
@@ -206,24 +227,34 @@
             tile(full * size, total % size)
         if k + 2 < count:
             w_copy(k + 2).start()
+        if k == 0:
+            out_copy.start()
 
     send_own(0)
     send_own(1)
+    send_own(2)
     own = pl.ds(pl.multiple_of(level * rows, rows), rows)
     meta_all[own, :] = meta_ref[...]
     for k in range(count):
         gathered[k][own, :] = normed_ref[:, starts[k] : starts[k] + cols[k][0]]
+    targets = slot_ref[0:1, :] + (level * PLANE).astype(f32)
+    sub = lax.broadcasted_iota(jnp.int32, (LANES, slot_ref.shape[1]), 0).astype(f32)
+    pick = jnp.where(sub == targets, 1.0, 0.0).astype(bf16)
+    gate_pick = jnp.where(sub == targets + LANES // 2, 1.0, 0.0).astype(bf16)
     relay(0)
     table = meta_all[...]
-    rank = jnp.dot(table, pick_ref[...], preferred_element_type=jnp.float32)
-    gate = jnp.dot(table, gate_ref[...], preferred_element_type=jnp.float32)
-    hit = rank == mark_ref[...]
-    combine[...] = jnp.where(hit, gate, 0.0).astype(jnp.bfloat16)
-    select[...] = jnp.transpose(jnp.where(hit, 1.0, 0.0)).astype(jnp.bfloat16)
+    rank = jnp.dot(table, pick, preferred_element_type=f32)
+    gate = jnp.dot(table, gate_pick, preferred_element_type=f32)
+    for z in range(depth):
+        there = slice(z * rows, (z + 1) * rows)
+        hit = (rank[there, :] == slot_ref[2:3, :]) & (slot_ref[1:2, :] == z)
+        combine[there, :] = jnp.where(hit, gate[there, :], 0.0).astype(bf16)
+        dense[there, : slot_ref.shape[1]] = jnp.where(hit, 1.0, 0.0)
+    select[...] = jnp.transpose(dense[:, : slot_ref.shape[1]]).astype(bf16)
 
     for k in range(count):
-        if k + 2 <= count:
-            send_own(k + 2)
+        if k + 3 <= count:
+            send_own(k + 3)
         relay(k + 1)
         sending[k][...] = jnp.dot(
             select[: PLANE * slots, :], gathered[k][...], preferred_element_type=jnp.float32
@@ -273,32 +304,42 @@
             tile(starts[k] + full * size, full * size, real % size)
         side_all(k, sending, answers, back_send, back_recv)
 
-    def ret(k, z, land, send, recv, target):
-        there = pl.ds(pl.multiple_of(z * rows, rows), rows)
+    def rows_of(z):
+        return pl.ds(pl.multiple_of(z * rows, rows), rows)
+
+    def ret(k, z, slot, target):
+        if slot is None:
+            dst, recv = relayed[k].at[rows_of(z), :], ret_recv.at[k, z]
+        else:
+            dst, recv = home_in[k].at[pl.ds(slot * rows, rows), :], home_recv.at[k, slot]
         return pltpu.make_async_remote_copy(
-            src_ref=gathered[k].at[there, :],
-            dst_ref=land[k].at[there, :],
-            send_sem=send.at[k, z],
-            recv_sem=recv.at[k, z],
+            src_ref=gathered[k].at[rows_of(z), :],
+            dst_ref=dst,
+            send_sem=ret_send.at[k, z],
+            recv_sem=recv,
             device_id={"ep": target},
             device_id_type=MESH,
         )
 
-    def pass_on(k, z, land, send, recv, target, more):
-        there = pl.ds(z * rows, rows)
-
-        @pl.when(more)
-        def _():
-            ret(k, z, land, send, recv, target).wait_recv()
-            gathered[k][there, :] = (
-                dense[there, : cols[k][0]] + land[k][there, :].astype(jnp.float32)
-            ).astype(jnp.bfloat16)
-
-        @pl.when(jnp.logical_not(more))
-        def _():
-            gathered[k][there, :] = dense[there, : cols[k][0]].astype(jnp.bfloat16)
-
-        ret(k, z, land, send, recv, target).start()
+    def pass_on(k, z, far, more, slot, target):
+        there = rows_of(z)
+        wide = cols[k][0]
+        if far > 1:
+
+            @pl.when(more)
+            def _():
+                ret(k, z, None, me).wait_recv()
+                gathered[k][there, :] = (
+                    dense[there, :wide] + relayed[k][there, :].astype(jnp.float32)
+                ).astype(jnp.bfloat16)
+
+            @pl.when(jnp.logical_not(more))
+            def _():
+                gathered[k][there, :] = dense[there, :wide].astype(jnp.bfloat16)
+
+        else:
+            gathered[k][there, :] = dense[there, :wide].astype(jnp.bfloat16)
+        ret(k, z, slot, target).start()
 
     def reduce(k):
         for step in range(1, PLANE):
@@ -307,43 +348,43 @@
         dense[:, :wide] = jnp.dot(
             combine[:, : PLANE * slots], answers[k][...], preferred_element_type=jnp.float32
         )
-        for far in range(depth - 1):
-            low, high = far, depth - 1 - far
-
-            @pl.when(low < level)
-            def _():
-                pass_on(k, low, from_above, ret_down_send, ret_down_recv, me - PLANE, has_up)
-
-            @pl.when(high > level)
-            def _():
-                pass_on(k, high, from_below, ret_up_send, ret_up_recv, me + PLANE, has_down)
+        for far in [*range(depth - 1, 2, -1), 1, 2]:
+            if far >= depth:
+                continue
+            low, high = level - far, level + far
+
+            @pl.when(low >= 0)
+            def _():
+                direct = far <= 2
+                hop = far if direct else 1
+                pass_on(k, low, far, has_up, far - 1 if direct else None, me - hop * PLANE)
+
+            @pl.when(high < depth)
+            def _():
+                direct = far <= 2
+                hop = far if direct else 1
+                pass_on(k, high, far, has_down, far + 1 if direct else None, me + hop * PLANE)
 
     def finish(k):
         wide, real = cols[k]
 
-        @pl.when(has_up)
-        def _():
-            ret(k, level, from_above, ret_down_send, ret_down_recv, me).wait_recv()
-
-        @pl.when(has_down)
-        def _():
-            ret(k, level, from_below, ret_up_send, ret_up_recv, me).wait_recv()
-
-        @pl.when(has_up)
-        def _():
-            home[k % 2, :, :wide] += from_above[k][own, :].astype(jnp.float32)
-
-        @pl.when(has_down)
-        def _():
-            home[k % 2, :, :wide] += from_below[k][own, :].astype(jnp.float32)
+        for slot, present, device in near:
+
+            @pl.when(present)
+            def _():
+                ret(k, level, slot, me).wait_recv()
+                home[k % 2, :, :wide] += home_in[k][slot * rows : (slot + 1) * rows, :].astype(
+                    jnp.float32
+                )
 
         here = slice(starts[k], starts[k] + real)
-        out_ref[:, here] = home[k % 2, :, :real] * inv_ref[...] + jnp.dot(
-            weight_ref[...],
+        moe = home[k % 2, :, :real] * inv + jnp.dot(
+            (gate_of * inv)[:, :experts],
             bias_out_ref[:, here],
-            preferred_element_type=jnp.float32,
+            preferred_element_type=f32,
             precision=lax.Precision.HIGHEST,
         )
+        out_ref[:, here] = (tokens_ref[:, here].astype(f32) + moe).astype(bf16)
 
     (home,) = take(1)
     for k in range(count):
@@ -365,13 +406,9 @@
             side(k, step, sending, answers, back_send, back_recv).wait_send()
         for z in range(depth):
 
-            @pl.when(z < level)
-            def _():
-                ret(k, z, from_above, ret_down_send, ret_down_recv, me - PLANE).wait_send()
-
-            @pl.when(z > level)
-            def _():
-                ret(k, z, from_below, ret_up_send, ret_up_recv, me + PLANE).wait_send()
+            @pl.when(z != level)
+            def _():
+                ret(k, z, None, me).wait_send()
 
 
 def fused(tokens, expert_ids, gate_ints, norm_gain, weight_in, bias_in, weight_out, bias_out):
@@ -390,37 +427,11 @@
     count = len(cols)
     lane_slots = round_up(PLANE * slots, LANES)
 
-    tok_float = tokens.astype(jnp.float32)
-    row_scale = lax.rsqrt(jnp.mean(tok_float * tok_float, axis=1, keepdims=True) + 1e-05)
-    normed = (tok_float * row_scale * norm_gain[None, :]).astype(jnp.bfloat16)
-    normed = jnp.pad(normed, ((0, 0), (0, padded - width)))
-    gates = gate_ints.astype(jnp.float32)
-    inv = 1.0 / jnp.sum(gates, axis=1, keepdims=True)
-    names = jnp.arange(experts, dtype=jnp.int32)
-    hot = expert_ids[:, :, None] == names[None, None, :]
-    chosen = jnp.any(hot, axis=1)
-    gate_of = jnp.sum(jnp.where(hot, gates[:, :, None], 0.0), axis=1)
-    expert_weight = gate_of * inv
-    lower = jnp.tril(jnp.ones((rows, rows), jnp.bfloat16))
-    rank = jnp.dot(lower, chosen.astype(jnp.bfloat16), preferred_element_type=jnp.float32)
-    rank = jnp.where(chosen, rank, 0.0)
-    gap = jnp.zeros((rows, LANES // 2 - experts), jnp.float32)
-    meta = jnp.concatenate([rank, gap, gate_of, gap], axis=1).astype(jnp.bfloat16)
-
-    level = lax.axis_index("ep") // PLANE
-    slot = jnp.arange(lane_slots, dtype=jnp.int32)
-    inside = slot % slots
-    target = level * PLANE + slot // slots
-    valid = (slot < PLANE * slots) & (inside < depth * CAP)
-    lane = jnp.arange(LANES, dtype=jnp.int32)[:, None]
-    pick = ((lane == target[None, :]) & valid[None, :]).astype(jnp.bfloat16)
-    gate_pick = ((lane == LANES // 2 + target[None, :]) & valid[None, :]).astype(jnp.bfloat16)
-    row_level = jnp.arange(depth * rows, dtype=jnp.int32)[:, None] // rows
-    mark = jnp.where(
-        valid[None, :] & (row_level == (inside // CAP)[None, :]),
-        (inside % CAP + 1)[None, :],
-        -1,
-    ).astype(jnp.float32)
+    table = np.full((8, lane_slots), -1000.0, np.float32)
+    for slot in range(PLANE * slots):
+        inside = slot % slots
+        if inside < depth * CAP:
+            table[:3, slot] = (slot // slots, inside // CAP, inside % CAP + 1)
 
     bf16, f32 = jnp.bfloat16, jnp.float32
     all_rows, all_slots = depth * rows, PLANE * slots
@@ -435,7 +446,7 @@
         + wide(all_slots)
         + wide(all_slots)
         + wide(all_rows)
-        + wide(all_rows)
+        + wide(4 * rows)
         + [
             pltpu.VMEM((all_rows, LANES), bf16),
             pltpu.VMEM((lane_slots, all_rows), bf16),
@@ -445,41 +456,40 @@
             pltpu.VMEM((all_slots, half), bf16),
             pltpu.VMEM((2, cols[0][0], 2 * half), bf16),
             pltpu.VMEM((half, width), bf16),
+            pltpu.VMEM((rows, padded), bf16),
+            pltpu.VMEM((rows, LANES), bf16),
             dma((count,)),
             dma,
-            dma((count + 1, depth)),
+            dma((count + 1, 4)),
             dma((count + 1, depth)),
             dma((count + 1, depth)),
         ]
         + [dma((count, PLANE))] * 4
-        + [dma((count, depth))] * 4
+        + [dma((count, depth)), dma((count, depth)), dma((count, 4))]
         + [pltpu.VMEM((2, rows, cols[0][0]), f32)]
     )
     vmem = pl.BlockSpec(memory_space=pltpu.VMEM)
     hbm = pl.BlockSpec(memory_space=pl.ANY)
-    moe = pl.pallas_call(
+    return pl.pallas_call(
         functools.partial(expert_kernel, (depth, rows, width, half, slots, cols)),
-        out_shape=jax.ShapeDtypeStruct((rows, width), f32),
-        in_specs=[vmem] * 9 + [hbm] * 2,
+        out_shape=jax.ShapeDtypeStruct((rows, width), bf16),
+        in_specs=[vmem] * 7 + [hbm] * 2,
         out_specs=vmem,
         scratch_shapes=scratch,
         compiler_params=pltpu.CompilerParams(
             collective_id=0, has_side_effects=True, vmem_limit_bytes=VMEM_ROOM
         ),
     )(
-        normed,
-        meta,
-        pick,
-        gate_pick,
-        mark,
-        inv,
-        expert_weight,
+        tokens,
+        expert_ids,
+        gate_ints,
+        norm_gain.reshape(1, width),
+        jnp.asarray(table),
         bias_out,
         bias_in,
         weight_in,
         weight_out,
     )
-    return (tok_float + moe).astype(jnp.bfloat16)
 
 
 def shards(tokens, expert_ids, gate_ints, norm_gain, weight_in, bias_in, weight_out, bias_out):

time: 125 us -> 97 us (0.78); the launches traced: 123 us -> 96.7 us
  Pallas kernels: 111 us -> 90.9 us
  other arithmetic: 10.1 us -> 0 us
  local copies, waits for them, and re-layouts: 1.75 us -> 5.82 us
    pallas_call x1, Pallas kernels: 111 us -> 90.9 us  [fused(): pl.pallas_call(functools.partial(expert_kernel, (depth, rows, width, half...]
    convert_element_type x5 -> x0, other arithmetic: 5.39 us -> none  [the longest x1 1.93 us: fused(): return (tok_float + moe).astype(jnp.bfloat16)]
    unnamed x2 -> x3, local copies, waits for them, and re-layouts: 0.01 us -> 4.51 us
    reduce_sum x3 -> x0, other arithmetic: 2.61 us -> none  [the longest x1 1.17 us: fused(): jnp.mean(tok_float * tok_float, axis=1, keepdims=True) + 1e-05]
    reshape x0 -> x1, local copies, waits for them, and re-layouts: none -> 1.31 us  [fused(): norm_gain.reshape(1, width)]
where the time goes in v2:
time: 97 us; the launch traced here: 96.7 us
  Pallas kernels  90.9 us (94%)
  local copies, waits for them, and re-layouts  5.82 us (6%)
    pallas_call x1, Pallas kernels, fused(): pl.pallas_call(functools.partial(expert_kernel, (depth, rows, width, half...  90.9 us
    unnamed x3, local copies, waits for them, and re-layouts  4.51 us

profile of v2, /device:TPU:0, one launch (start us, length us, event | category | flops | bytes accessed | tf_op | source)
XLA Modules:
  0.0 96.7 jit_solution(8723977103424786500)
XLA Ops:
  0.0 1.3 %reshape.3.gain_ref = f32[1,2880]{1,0:T(1,128)} reshape(f32[2880]{0:T(1024)} %param.12) | data formatting | bytes 23040 | tf_op jit(solution)/shard_map/reshape | solution.py:486
  1.3 1.4 %copy.10.ids_ref = s32[64,4]{1,0:T(8,128)} copy(s32[64,4]{0,1:T(4,128)} %param.10) | data formatting | bytes 2048 | tf_op args[1]
  2.7 1.4 %copy.11.gates_ref = s32[64,4]{1,0:T(8,128)} copy(s32[64,4]{0,1:T(4,128)} %param.11) | data formatting | bytes 2048 | tf_op args[2]
  4.1 90.9 %shard_map.91 = bf16[64,2880]{1,0:T(8,128)(2,1)} custom-call(bf16[64,2880]{1,0:T(8,128)(2,1)} %tokens_ref.1, s32[64,4]{1,0:T(8,128)} %copy.10.ids_ref, s32[64,4]{1,0:T(8,128)} %copy.11.gates_ref, f32[1,2880]{1,0:T(1,128)} %reshape.3.gain_ref, f32[8,384]{1,0:T(8,128)} %constant.2.clone.slot_ref, f32[16,2880]{1,0:T(8,128)} %bias_out_ref.1, ...), custom_call_target="tpu_custom_call" | custom-call | tf_op jit(solution)/shard_map/pallas_call | solution.py:473
  95.0 1.8 %copy.13 = bf16[64,2880]{1,0:T(8,128)(2,1)} copy(bf16[64,2880]{1,0:T(8,128)(2,1)} %shard_map.91) | data formatting | bytes 737280

commit v3 on v2

--- a/solution.py
+++ b/solution.py
@@ -216,7 +216,7 @@
                 acc[:, pl.ds(start, size)] += part
 
         total = 2 * half
-        size = 512
+        size = 1152
         full = total // size
 
         @pl.loop(0, full)

time: 97 us -> 95.6 us (0.986)
  Pallas kernels: 90.9 us -> 89.5 us
    pallas_call x1, Pallas kernels: 90.9 us -> 89.5 us  [fused(): pl.pallas_call(functools.partial(expert_kernel, (depth, rows, width, half...]
where the time goes in v3:
time: 95.6 us; the launch traced here: 95.4 us
  Pallas kernels  89.5 us (94%)
  local copies, waits for them, and re-layouts  5.82 us (6%)
    pallas_call x1, Pallas kernels, fused(): pl.pallas_call(functools.partial(expert_kernel, (depth, rows, width, half...  89.5 us
    unnamed x3, local copies, waits for them, and re-layouts  4.51 us

profile of v3, /device:TPU:0, one launch (start us, length us, event | category | flops | bytes accessed | tf_op | source)
XLA Modules:
  0.0 95.4 jit_solution(7620509152118117788)
XLA Ops:
  0.0 1.3 %reshape.3.gain_ref = f32[1,2880]{1,0:T(1,128)} reshape(f32[2880]{0:T(1024)} %param.12) | data formatting | bytes 23040 | tf_op jit(solution)/shard_map/reshape | solution.py:486
  1.3 1.4 %copy.10.ids_ref = s32[64,4]{1,0:T(8,128)} copy(s32[64,4]{0,1:T(4,128)} %param.10) | data formatting | bytes 2048 | tf_op args[1]
  2.7 1.4 %copy.11.gates_ref = s32[64,4]{1,0:T(8,128)} copy(s32[64,4]{0,1:T(4,128)} %param.11) | data formatting | bytes 2048 | tf_op args[2]
  4.1 89.5 %shard_map.91 = bf16[64,2880]{1,0:T(8,128)(2,1)} custom-call(bf16[64,2880]{1,0:T(8,128)(2,1)} %tokens_ref.1, s32[64,4]{1,0:T(8,128)} %copy.10.ids_ref, s32[64,4]{1,0:T(8,128)} %copy.11.gates_ref, f32[1,2880]{1,0:T(1,128)} %reshape.3.gain_ref, f32[8,384]{1,0:T(8,128)} %constant.2.clone.slot_ref, f32[16,2880]{1,0:T(8,128)} %bias_out_ref.1, ...), custom_call_target="tpu_custom_call" | custom-call | tf_op jit(solution)/shard_map/pallas_call | solution.py:473
  93.6 1.8 %copy.13 = bf16[64,2880]{1,0:T(8,128)(2,1)} copy(bf16[64,2880]{1,0:T(8,128)(2,1)} %shard_map.91) | data formatting | bytes 737280
